TPU v7x, 512 devices: a whole 4x8x8 slice. The times are simulated.
512 devices in a mesh: xi: 32 (over x, z), eta: 16 (over y, core).
Axes of the slice: x: 4, y: 8, z: 8, core: 2. Of those that a mesh axis runs over, the one named last changes fastest.
Arguments:
- residual: float32 [5, 2048, 2048], P(None, 'xi', 'eta'), may hold values from -30 to 30
- left_eta: float32 [5, 5, 2048, 2048], P(None, None, 'xi', 'eta'), may hold values from -2.7 to 2.7
- middle: float32 [5, 5, 2048, 2048], P(None, None, 'xi', 'eta'), may hold values from -2.7 to 2.7
- right_xi: float32 [5, 5, 2048, 2048], P(None, None, 'xi', 'eta'), may hold values from -2.7 to 2.7
- speed_eta: float32 [5, 2048, 2048], P(None, 'xi', 'eta'), may hold values from -120.25 to 120.25
- speed_xi: float32 [5, 2048, 2048], P(None, 'xi', 'eta'), may hold values from -120.25 to 120.25
- damping_eta: float32 [2048, 2048], P('xi', 'eta'), may hold values from 0.5 to 3
- damping_xi: float32 [2048, 2048], P('xi', 'eta'), may hold values from 0.5 to 3
Outputs:
- increment: float32 [5, 2048, 2048], P(None, 'xi', 'eta')
All inputs are finite; a program needn't handle non-finite values.
Results may differ from a plain program's by a relative error of at most 0.000041.
Values sent between devices are 32-bit elements; how exact they have to be, the bound alone decides.
No kernel may reach another device: no remote copies, remote signals or barrier semaphores. Data moves between devices by JAX's collectives and lax.ppermute only.
A program may use at most 128 MiB of HBM per device.

v0:
```python
import functools

import jax
import jax.numpy as jnp
from jax import lax
from jax.experimental import pallas as pl
from jax.experimental.pallas import tpu as pltpu
from jax.sharding import PartitionSpec as P

SPAN = 2
FIELDS = 5
STEPS = 8
LANES = 128
FORM = 20
SENT = 24


def merge(low, high):
    a_p0, a_p1, a_q0, a_q1 = (low[5 * x : 5 * x + 5] for x in range(4))
    b_p0, b_p1, b_q0, b_q1 = (high[5 * x : 5 * x + 5] for x in range(4))
    l00, l01, l10, l11 = b_p0[1], b_p0[2], b_p1[1], b_p1[2]
    u00, u01, u10, u11 = a_q0[3], a_q0[4], a_q1[3], a_q1[4]
    m00 = 1.0 - l00 * u00 - l01 * u10
    m01 = -(l00 * u01 + l01 * u11)
    m10 = -(l10 * u00 + l11 * u10)
    m11 = 1.0 - l10 * u01 - l11 * u11
    inv = 1.0 / (m00 * m11 - m01 * m10)
    m00, m01, m10, m11 = m00 * inv, m01 * inv, m10 * inv, m11 * inv
    r0 = [b_p0[0] - l00 * a_q0[0] - l01 * a_q1[0]]
    r1 = [b_p1[0] - l10 * a_q0[0] - l11 * a_q1[0]]
    for c in (1, 2):
        r0.append(-(l00 * a_q0[c] + l01 * a_q1[c]))
        r1.append(-(l10 * a_q0[c] + l11 * a_q1[c]))
    r0 += [b_p0[3], b_p0[4]]
    r1 += [b_p1[3], b_p1[4]]
    p0 = [m11 * s - m01 * t for s, t in zip(r0, r1)]
    p1 = [m00 * t - m10 * s for s, t in zip(r0, r1)]

    def through_p(row):
        out = [row[c] - row[3] * p0[c] - row[4] * p1[c] for c in (0, 1, 2)]
        return out + [-(row[3] * p0[c] + row[4] * p1[c]) for c in (3, 4)]

    q0, q1 = through_p(a_q0), through_p(a_q1)

    def through_q(row):
        out = [row[0] - row[1] * q0[0] - row[2] * q1[0]]
        out += [-(row[1] * q0[c] + row[2] * q1[c]) for c in (1, 2)]
        return out + [row[c] - row[1] * q0[c] - row[2] * q1[c] for c in (3, 4)]

    joined = through_p(a_p0) + through_p(a_p1) + through_q(b_q0) + through_q(b_q1)
    return joined, p0 + p1 + q0 + q1


def value_of(row, outside):
    return (row[0] - row[1] * outside[0] - row[2] * outside[1]) - (
        row[3] * outside[2] + row[4] * outside[3]
    )


def plain_form(form, damp_low, speed_low, damp_high, speed_high):
    turn_low = 2.0 * damp_low + 0.5 * speed_low
    turn_high = 0.5 * speed_high - 2.0 * damp_high
    rows = []
    for x in range(4):
        k, a, b, c, d = form[5 * x : 5 * x + 5]
        rows.append([k, a * damp_low, b - a * turn_low, c + d * turn_high, d * damp_high])
    first, last = rows[0], rows[3]
    e00, e01 = 1.0 + first[1], first[4]
    e10, e11 = last[1], 1.0 + last[4]
    inv = 1.0 / (e00 * e11 - e01 * e10)
    e00, e01, e10, e11 = e00 * inv, e01 * inv, e10 * inv, e11 * inv
    new_first = [e11 * s - e01 * t for s, t in zip(first, last)]
    new_last = [e00 * t - e10 * s for s, t in zip(first, last)]
    inner = [
        [row[c] - row[1] * new_first[c] - row[4] * new_last[c] for c in range(5)]
        for row in rows[1:3]
    ]
    return new_first + inner[0] + inner[1] + new_last


def rim_terms(outside, first, last, damp_low, speed_low, damp_high, speed_high):
    l0, l1, r0, r1 = outside
    low = damp_low * (l0 - 2.0 * l1 + first) - 0.5 * speed_low * l1
    high = damp_high * (last - 2.0 * r0 + r1) + 0.5 * speed_high * r0
    return [low, l1, r0, high]


def section_rows():
    return lax.broadcasted_iota(jnp.int32, (STEPS, LANES), 0)


def reduce_sections(values, speeds, damps, cols_ref, form_ref):
    row = section_rows()
    zero = jnp.zeros((STEPS, LANES), jnp.float32)

    def below(x):
        return jnp.where(row == 0, zero, pltpu.roll(x, 1, 0))

    def above(x):
        return jnp.where(row == STEPS - 1, zero, pltpu.roll(x, STEPS - 1, 0))

    damp = [damps(j) for j in range(STEPS)]
    damp = [below(damp[-1])] + damp + [above(damp[0])]
    edge = [2.0 * (damp[j] + damp[j + 1]) for j in range(STEPS + 1)]
    centre = [1.0 + damp[j] + 4.0 * damp[j + 1] + damp[j + 2] for j in range(STEPS)]
    far_first = jnp.where(row == 0, 1.0, damp[0])
    far_last = jnp.where(row == STEPS - 1, 1.0, damp[STEPS + 1])
    for f in range(FIELDS):
        half = [0.5 * speeds(f, j) for j in range(STEPS)]
        half = [below(half[-1])] + half + [above(half[0])]
        parts = []
        for j in range(STEPS):
            far_low = damp[j]
            near_low = -(half[j] + edge[j])
            near_up = half[j + 2] - edge[j + 1]
            far_up = far_last if j == STEPS - 1 else damp[j + 2]
            source = values(f, j)
            if j == 0:
                inv = 1.0 / centre[0]
                parts.append(
                    [source * inv, far_first * inv, near_low * inv, near_up * inv, far_up * inv]
                )
                continue
            k1, a1, b1, n1, m1 = parts[j - 1]
            if j == 1:
                inv = 1.0 / (centre[1] - near_low * n1)
                parts.append(
                    [
                        (source - near_low * k1) * inv,
                        -(near_low * a1) * inv,
                        (far_low - near_low * b1) * inv,
                        (near_up - near_low * m1) * inv,
                        far_up * inv,
                    ]
                )
                continue
            k2, a2, b2, n2, m2 = parts[j - 2]
            lead = near_low - far_low * n2
            inv = 1.0 / ((centre[j] - far_low * m2) - lead * n1)
            parts.append(
                [
                    ((source - far_low * k2) - lead * k1) * inv,
                    -(far_low * a2 + lead * a1) * inv,
                    -(far_low * b2 + lead * b1) * inv,
                    (near_up - lead * m1) * inv,
                    far_up * inv,
                ]
            )
        cols = [None] * STEPS
        cols[7] = parts[7]
        k, a, b, n, m = parts[6]
        nxt = cols[7]
        cols[6] = [
            k - n * nxt[0],
            a - n * nxt[1],
            b - n * nxt[2],
            m - n * nxt[3],
            -(n * nxt[4]),
        ]
        for j in range(STEPS - 3, -1, -1):
            k, a, b, n, m = parts[j]
            nxt, aft = cols[j + 1], cols[j + 2]
            cols[j] = [
                k - n * nxt[0] - m * aft[0],
                a - n * nxt[1] - m * aft[1],
                b - n * nxt[2] - m * aft[2],
                -(n * nxt[3] + m * aft[3]),
                -(n * nxt[4] + m * aft[4]),
            ]
        for j in range(STEPS):
            for c in range(5):
                cols_ref[c, f, j] = cols[j][c]
        for x, j in enumerate((0, 1, STEPS - 2, STEPS - 1)):
            for c in range(5):
                form_ref[5 * x + c, pl.ds(STEPS * f, STEPS), :] = cols[j][c]


def merge_rows(src_ref, count, meet_ref):
    low = [src_ref[v, pl.ds(0, count, stride=2), :] for v in range(FORM)]
    high = [src_ref[v, pl.ds(1, count, stride=2), :] for v in range(FORM)]
    joined, meet = merge(low, high)
    for v in range(FORM):
        meet_ref[v] = meet[v]
    return joined


def merge_tree(form_ref, mid_ref, small_ref, meets):
    for v, item in enumerate(merge_rows(form_ref, 20, meets[0])):
        mid_ref[v] = item
    for v, item in enumerate(merge_rows(mid_ref, 10, meets[1])):
        small_ref[v] = item
    return merge_rows(small_ref, 5, meets[2])


def spread_tree(outside, meets, spreads):
    for meet_ref, out_ref, count in zip(meets[::-1], spreads, (5, 10, 20)):
        p0, p1, q0, q1 = (
            value_of([meet_ref[5 * x + c] for c in range(5)], outside) for x in range(4)
        )
        even = (outside[0], outside[1], p0, p1)
        odd = (q0, q1, outside[2], outside[3])
        for x in range(4):
            out_ref[x, pl.ds(0, count, stride=2), :] = even[x]
            out_ref[x, pl.ds(1, count, stride=2), :] = odd[x]
        outside = [out_ref[x] for x in range(4)]


def section_values(cols_ref, spread_ref, f, j):
    outside = [spread_ref[x, pl.ds(STEPS * f, STEPS), :] for x in range(4)]
    return value_of([cols_ref[c, f, j] for c in range(5)], outside)


def apply_cells(matrix_ref, values, out_ref):
    for f in range(FIELDS):
        total = matrix_ref[f, 0] * values[0]
        for g in range(1, FIELDS):
            total = total + matrix_ref[f, g] * values[g]
        out_ref[f] = total


def rim_rows(first, last):
    return [first[0], first[1], last[0], last[1]]


def to_eta_rows(block):
    beside = pltpu.roll(block, LANES - 1, 1)
    return jnp.transpose(jnp.concatenate([block, beside], axis=0))


def from_eta_rows(rows):
    both = jnp.transpose(rows)
    half = both.shape[0] // 2
    lane = lax.broadcasted_iota(jnp.int32, (half, LANES), 1)
    return jnp.where(lane % 2 == 0, both[:half], pltpu.roll(both[half:], 1, 1))


def eta_reduce_kernel(
    residual_ref, left_ref, speed_ref, damp_ref,
    send_ref, cols_ref, meet0_ref, meet1_ref, meet2_ref,
    work_ref, turned_ref, form_ref, mid_ref, small_ref,
):
    apply_cells(left_ref, [residual_ref[g] for g in range(FIELDS)], work_ref)
    for f in range(FIELDS):
        turned_ref[f] = to_eta_rows(work_ref[f])
        turned_ref[FIELDS + f] = to_eta_rows(speed_ref[f])
    turned_ref[2 * FIELDS] = to_eta_rows(damp_ref[...])

    def cell(index, j):
        return turned_ref[index, pl.ds(SPAN * j, STEPS, stride=SPAN * STEPS), :]

    reduce_sections(
        cell,
        lambda f, j: cell(FIELDS + f, j),
        lambda j: cell(2 * FIELDS, j),
        cols_ref,
        form_ref,
    )
    block = merge_tree(form_ref, mid_ref, small_ref, (meet0_ref, meet1_ref, meet2_ref))
    for v in range(FORM):
        send_ref[pl.ds(FIELDS * v, FIELDS), :] = block[v]
    final = SPAN * (STEPS * STEPS - 1)
    for f in range(FIELDS):
        rims = (
            turned_ref[2 * FIELDS, pl.ds(0, 1), :],
            turned_ref[FIELDS + f, pl.ds(0, 1), :],
            turned_ref[2 * FIELDS, pl.ds(final, 1), :],
            turned_ref[FIELDS + f, pl.ds(final, 1), :],
        )
        for r in range(4):
            send_ref[pl.ds(FIELDS * (FORM + r) + f, 1), :] = rims[r]


def eta_outside(place_ref, got_ref, form_ref, mid_ref, small_ref, meets, spreads, all_ref, own_ref):
    row = section_rows()
    zero = jnp.zeros((STEPS, LANES), jnp.float32)
    rows_each = SENT * FIELDS
    pair_forms, pair_meets, rims = [], [], []
    for f in range(FIELDS):
        halves = [
            [
                got_ref[pl.ds(rows_each * side + FIELDS * v + f, STEPS, stride=2 * rows_each), :]
                for v in range(SENT)
            ]
            for side in range(2)
        ]
        even, odd = halves
        rim_even = (
            jnp.where(row == 0, zero, pltpu.roll(odd[22], 1, 0)),
            jnp.where(row == 0, zero, pltpu.roll(odd[23], 1, 0)),
            odd[20],
            odd[21],
        )
        rim_odd = (
            even[22],
            even[23],
            jnp.where(row == STEPS - 1, zero, pltpu.roll(even[20], STEPS - 1, 0)),
            jnp.where(row == STEPS - 1, zero, pltpu.roll(even[21], STEPS - 1, 0)),
        )
        low = plain_form(even[:FORM], *rim_even)
        high = plain_form(odd[:FORM], *rim_odd)
        joined, meet = merge(low, high)
        for v in range(FORM):
            form_ref[v, pl.ds(STEPS * f, STEPS), :] = joined[v]
        pair_meets.append(meet)
        pair_forms.append((low[:5], low[15:], high[:5], high[15:]))
        rims.append((rim_even, rim_odd))
    merge_tree(form_ref, mid_ref, small_ref, meets)
    nothing = jnp.zeros((FIELDS, LANES), jnp.float32)
    spread_tree([nothing] * 4, meets, spreads)
    place = place_ref[0]
    for f in range(FIELDS):
        l0, l1, r0, r1 = (spreads[2][x, pl.ds(STEPS * f, STEPS), :] for x in range(4))
        p0, p1, q0, q1 = (
            value_of(pair_meets[f][5 * x : 5 * x + 5], (l0, l1, r0, r1)) for x in range(4)
        )
        for side, around in enumerate(((l0, l1, p0, p1), (q0, q1, r0, r1))):
            first = value_of(pair_forms[f][2 * side], around)
            last = value_of(pair_forms[f][2 * side + 1], around)
            for x, item in enumerate(rim_terms(around, first, last, *rims[f][side])):
                all_ref[x, side, pl.ds(STEPS * f, STEPS), :] = item
        side = lax.rem(place, 2)
        pair = lax.div(place, 2)
        for x in range(4):
            own_ref[x, pl.ds(f, 1), :] = all_ref[x, side, pl.ds(STEPS * f + pair, 1), :]


def eta_finish_kernel(
    place_ref, got_ref, eta_cols_ref, eta_meet0_ref, eta_meet1_ref, eta_meet2_ref,
    middle_ref, speed_ref, damp_ref,
    send_ref, cols_ref, meet0_ref, meet1_ref, meet2_ref,
    form_ref, mid_ref, small_ref, spread0_ref, spread1_ref, spread2_ref, all_ref, own_ref,
    turned_ref, mixed_ref, square_ref,
):
    spreads = (spread0_ref, spread1_ref, spread2_ref)
    meets = (meet0_ref, meet1_ref, meet2_ref)
    eta_outside(place_ref, got_ref, form_ref, mid_ref, small_ref, meets, spreads, all_ref, own_ref)
    spread_tree(
        [own_ref[x] for x in range(4)], (eta_meet0_ref, eta_meet1_ref, eta_meet2_ref), spreads
    )
    solved = []
    for f in range(FIELDS):
        for j in range(STEPS):
            turned_ref[f, pl.ds(SPAN * j, STEPS, stride=SPAN * STEPS), :] = section_values(
                eta_cols_ref, spread2_ref, f, j
            )
        solved.append(from_eta_rows(turned_ref[f]))
    apply_cells(middle_ref, solved, mixed_ref)
    reduce_sections(
        lambda f, j: mixed_ref[f, pl.ds(j, STEPS, stride=STEPS), :],
        lambda f, j: speed_ref[f, pl.ds(j, STEPS, stride=STEPS), :],
        lambda j: damp_ref[pl.ds(j, STEPS, stride=STEPS), :],
        cols_ref,
        form_ref,
    )
    block = merge_tree(form_ref, mid_ref, small_ref, meets)
    for v in range(FORM):
        square_ref[pl.ds(FIELDS * v, FIELDS), :] = block[v]
    final = STEPS * STEPS - 1
    for f in range(FIELDS):
        rims = (
            damp_ref[pl.ds(0, 1), :],
            speed_ref[f, pl.ds(0, 1), :],
            damp_ref[pl.ds(final, 1), :],
            speed_ref[f, pl.ds(final, 1), :],
        )
        for r in range(4):
            square_ref[pl.ds(FIELDS * (FORM + r) + f, 1), :] = rims[r]
    square_ref[pl.ds(SENT * FIELDS, LANES - SENT * FIELDS), :] = jnp.zeros(
        (LANES - SENT * FIELDS, LANES), jnp.float32
    )
    send_ref[...] = jnp.transpose(square_ref[...])


def xi_loop_kernel(got_ref, send_ref, square_ref):
    square_ref[...] = jnp.transpose(got_ref[...])
    items = [square_ref[pl.ds(FIELDS * v, FIELDS), :] for v in range(SENT)]
    width = 4

    def from_below(x, distance):
        return pltpu.roll(x, width * distance, 1)

    def from_above(x, distance):
        return pltpu.roll(x, LANES - width * distance, 1)

    rims = (
        from_below(items[22], 1),
        from_below(items[23], 1),
        from_above(items[20], 1),
        from_above(items[21], 1),
    )
    form = plain_form(items[:FORM], *rims)
    distance = 1
    while width * distance < LANES:
        form, unused = merge(form, [from_above(x, distance) for x in form])
        distance = 2 * distance
    unknown = [[None] * 5 for _ in range(4)]
    for x in range(4):
        k, a, b, c, d = form[5 * x : 5 * x + 5]
        unknown[x] = [c, d, a, b, k]
        unknown[x][x] = 1.0 + unknown[x][x]
    for pivot in range(4):
        inv = 1.0 / unknown[pivot][pivot]
        scaled = [unknown[pivot][c] * inv for c in range(pivot + 1, 5)]
        for x in range(4):
            if x == pivot:
                continue
            factor = unknown[x][pivot]
            for c in range(pivot + 1, 5):
                unknown[x][c] = unknown[x][c] - factor * scaled[c - pivot - 1]
        for c in range(pivot + 1, 5):
            unknown[pivot][c] = scaled[c - pivot - 1]
    p0, p1, l0, l1 = (unknown[x][4] for x in range(4))
    r0, r1 = from_above(p0, 1), from_above(p1, 1)
    terms = rim_terms([l0, l1, r0, r1], p0, from_above(l1, 1), *rims)
    square_ref[...] = jnp.zeros((LANES, LANES), jnp.float32)
    for x in range(4):
        square_ref[pl.ds(FIELDS * x, FIELDS), :] = terms[x]
    send_ref[...] = jnp.transpose(square_ref[...])


def xi_finish_kernel(
    got_ref, cols_ref, meet0_ref, meet1_ref, meet2_ref, right_ref,
    out_ref,
    square_ref, spread0_ref, spread1_ref, spread2_ref, solved_ref,
):
    square_ref[...] = jnp.transpose(got_ref[...])
    outside = [square_ref[pl.ds(FIELDS * x, FIELDS), :] for x in range(4)]
    spread_tree(
        outside, (meet0_ref, meet1_ref, meet2_ref), (spread0_ref, spread1_ref, spread2_ref)
    )
    for f in range(FIELDS):
        for j in range(STEPS):
            solved_ref[f, pl.ds(j, STEPS, stride=STEPS), :] = section_values(
                cols_ref, spread2_ref, f, j
            )
    apply_cells(right_ref, [solved_ref[g] for g in range(FIELDS)], out_ref)


def shape(*dims):
    return jax.ShapeDtypeStruct(dims, jnp.float32)


def vmem(*dims):
    return pltpu.VMEM(dims, jnp.float32)


KEPT = (
    shape(5, FIELDS, STEPS, STEPS, LANES),
    shape(FORM, 20, LANES),
    shape(FORM, 10, LANES),
    shape(FORM, 5, LANES),
)
FORMS = (vmem(FORM, 40, LANES), vmem(FORM, 20, LANES), vmem(FORM, 10, LANES))
SPREADS = (vmem(4, 10, LANES), vmem(4, 20, LANES), vmem(4, 40, LANES))


def call(kernel, outs, scratch, name, scalars=0):
    def run(*args):
        specs = [pl.BlockSpec(memory_space=pltpu.SMEM)] * scalars
        specs += [pl.BlockSpec(memory_space=pltpu.VMEM)] * (len(args) - scalars)
        out_specs = [pl.BlockSpec(memory_space=pltpu.VMEM)] * len(outs)
        return pl.pallas_call(
            kernel,
            out_shape=list(outs),
            in_specs=specs,
            out_specs=out_specs,
            scratch_shapes=list(scratch),
            compiler_params=pltpu.CompilerParams(vmem_limit_bytes=24 * 2**20),
            name=name,
        )(*args)

    return run


def per_device(residual, left_eta, middle, right_xi, speed_eta, speed_xi, damping_eta, damping_xi):
    fields, cells_xi, cells_local = residual.shape
    eta_send, *eta_kept = call(
        eta_reduce_kernel,
        (shape(SENT * FIELDS, LANES),) + KEPT,
        (vmem(FIELDS, cells_xi, LANES), vmem(2 * FIELDS + 1, LANES, LANES)) + FORMS,
        "eta_reduce",
    )(residual, left_eta, speed_eta, damping_eta)
    eta_got = lax.all_gather(eta_send, "eta", axis=0, tiled=True)
    place = lax.axis_index("eta").reshape(1).astype(jnp.int32)
    xi_send, *xi_kept = call(
        eta_finish_kernel,
        (shape(LANES, LANES),) + KEPT,
        FORMS
        + SPREADS
        + (
            vmem(4, 2, 40, LANES),
            vmem(4, FIELDS, LANES),
            vmem(FIELDS, LANES, LANES),
            vmem(FIELDS, cells_xi, LANES),
            vmem(LANES, LANES),
        ),
        "eta_finish",
        scalars=1,
    )(place, eta_got, *eta_kept, middle, speed_xi, damping_xi)
    loop = lax.axis_size("xi")
    xi_got = lax.all_to_all(
        xi_send.reshape(loop, LANES // loop, LANES), "xi", 0, 0, tiled=True
    ).reshape(LANES, LANES)
    (loop_send,) = call(xi_loop_kernel, (shape(LANES, LANES),), (vmem(LANES, LANES),), "xi_loop")(
        xi_got
    )
    loop_got = lax.all_to_all(
        loop_send.reshape(loop, LANES // loop, LANES), "xi", 0, 0, tiled=True
    ).reshape(LANES, LANES)
    (increment,) = call(
        xi_finish_kernel,
        (shape(fields, cells_xi, cells_local),),
        (vmem(LANES, LANES),) + SPREADS + (vmem(FIELDS, cells_xi, LANES),),
        "xi_finish",
    )(loop_got, *xi_kept, right_xi)
    return increment


def solution(mesh):
    in_specs = (
        P(None, "xi", "eta"),
        P(None, None, "xi", "eta"),
        P(None, None, "xi", "eta"),
        P(None, None, "xi", "eta"),
        P(None, "xi", "eta"),
        P(None, "xi", "eta"),
        P("xi", "eta"),
        P("xi", "eta"),
    )
    out_specs = P(None, "xi", "eta")
    return jax.shard_map(
        per_device, mesh=mesh, in_specs=in_specs, out_specs=out_specs, check_vma=False
    )
```

profile of v0, /device:TPU:2, one launch (start us, length us, event | category | flops | bytes accessed | tf_op | source)
XLA Modules:
  0.0 63.9 jit_solution(3777483856563535487)
XLA Ops:
  0.0 0.0 copy-start
  0.0 1.1 %copy-done = f32[5,5,64,128]{3,2,1,0:T(8,128)S(1)} copy-done((f32[5,5,64,128]{3,2,1,0:T(8,128)S(1)}, f32[5,5,64,128]{3,2,1,0:T(8,128)}, u32[]{:S(2)}) %copy-start) | copy-done | bytes 819224
  1.1 0.0 copy-start.4
  1.1 0.9 %copy-done.4 = f32[5,64,128]{2,1,0:T(8,128)S(1)} copy-done((f32[5,64,128]{2,1,0:T(8,128)S(1)}, f32[5,64,128]{2,1,0:T(8,128)}, u32[]{:S(2)}) %copy-start.4) | copy-done | bytes 163864
  2.1 0.0 copy-start.5
  2.1 0.9 %copy-done.5 = f32[5,64,128]{2,1,0:T(8,128)S(1)} copy-done((f32[5,64,128]{2,1,0:T(8,128)S(1)}, f32[5,64,128]{2,1,0:T(8,128)}, u32[]{:S(2)}) %copy-start.5) | copy-done | bytes 163864
  3.0 0.0 copy-start.7
  3.0 0.8 %copy-done.7 = f32[64,128]{1,0:T(8,128)S(1)} copy-done((f32[64,128]{1,0:T(8,128)S(1)}, f32[64,128]{1,0:T(8,128)}, u32[]{:S(2)}) %copy-start.7) | copy-done | bytes 32792
  3.7 0.8 %eta_reduce.1 = (f32[120,128]{1,0:T(8,128)S(1)}, f32[5,5,8,8,128]{4,3,2,1,0:T(8,128)S(1)}, f32[20,20,128]{2,1,0:T(8,128)S(1)}, f32[20,10,128]{2,1,0:T(8,128)S(1)}, f32[20,5,128]{2,1,0:T(8,128)S(1)}) custom-call(f32[5,64,128]{2,1,0:T(8,128)S(1)} %copy-done.4, f32[5,5,64,128]{3,2,1,0:T(8,128)S(1)} %copy-done, f32[5,64,128]{2,1,0:T(8,128)S(1)} %copy-done.5, ...), custom_call_target="tpu_custom_call" | custom-call | tf_op jit(solution)/shard_map/eta_reduce/pallas_call | solution.py:462
  4.5 0.0 copy-start.1
  4.6 0.0 copy-start.3
  4.6 0.0 copy-start.6
  4.6 20.4 %all_gather.3.got_ref = f32[1920,128]{1,0:T(8,128)S(1)} all-gather(f32[120,128]{1,0:T(8,128)S(1)} %get-tuple-element.15), channel_id=1, replica_groups=mesh['xi'=32,'eta'=16] {'eta'}, dimensions={0}, use_global_device_ids=true | all-gather | bytes 1044480 | tf_op jit(solution)/shard_map/all_gather | solution.py:483
  25.0 0.0 copy-done.1
  25.0 0.0 copy-done.3
  25.0 0.0 copy-done.6
  25.0 0.0 copy-start.2
  25.0 1.8 %eta_finish.1 = (f32[128,128]{1,0:T(8,128)S(1)}, f32[5,5,8,8,128]{4,3,2,1,0:T(8,128)S(1)}, f32[20,20,128]{2,1,0:T(8,128)S(1)}, f32[20,10,128]{2,1,0:T(8,128)S(1)}, f32[20,5,128]{2,1,0:T(8,128)S(1)}) custom-call(s32[1]{0:T(128)} %bitcast.place_ref, f32[1920,128]{1,0:T(8,128)S(1)} %all_gather.3.got_ref, ...), custom_call_target="tpu_custom_call" | custom-call | tf_op jit(solution)/shard_map/eta_finish/pallas_call | solution.py:462
  26.8 22.1 %all_to_all.10 = f32[32,4,128]{2,1,0:T(4,128)S(1)} all-to-all(f32[32,4,128]{2,1,0:T(4,128)S(1)} %bitcast.8), channel_id=1, replica_groups=mesh['xi'=32,'eta'=16] {'xi'}, dimensions={0} | all-to-all | bytes 131072 | tf_op jit(solution)/shard_map/all_to_all | solution.py:501
  48.9 0.9 %xi_loop.1 = f32[128,128]{1,0:T(8,128)S(1)} custom-call(f32[128,128]{1,0:T(8,128)S(1)} %bitcast.6), custom_call_target="tpu_custom_call" | custom-call | tf_op jit(solution)/shard_map/xi_loop/pallas_call | solution.py:462
  49.8 13.2 %all_to_all.11 = f32[32,4,128]{2,1,0:T(4,128)S(1)} all-to-all(f32[32,4,128]{2,1,0:T(4,128)S(1)} %bitcast.7), channel_id=1, replica_groups=mesh['xi'=32,'eta'=16] {'xi'}, dimensions={0} | all-to-all | bytes 131072 | tf_op jit(solution)/shard_map/all_to_all | solution.py:507
  63.0 0.0 copy-done.2
  63.0 0.9 %xi_finish.1 = f32[5,64,128]{2,1,0:T(8,128)} custom-call(f32[128,128]{1,0:T(8,128)S(1)} %bitcast.5, f32[5,5,8,8,128]{4,3,2,1,0:T(8,128)S(1)} %get-tuple-element.21.cols_ref, f32[20,20,128]{2,1,0:T(8,128)S(1)} %get-tuple-element.22.meet0_ref, f32[20,10,128]{2,1,0:T(8,128)S(1)} %get-tuple-element.23.meet1_ref, f32[20,5,128]{2,1,0:T(8,128)S(1)} %get-tuple-element.24.meet2_ref, ...), custom_call_target="tpu_custom_call" | custom-call | tf_op jit(solution)/shard_map/xi_finish/pallas_call | solution.py:462
Async XLA Ops:
  0.0 1.1 %copy-start = (f32[5,5,64,128]{3,2,1,0:T(8,128)S(1)}, f32[5,5,64,128]{3,2,1,0:T(8,128)}, u32[]{:S(2)}) copy-start(f32[5,5,64,128]{3,2,1,0:T(8,128)} %left_ref.1) | copy-start | bytes 2457604
  1.1 0.9 %copy-start.4 = (f32[5,64,128]{2,1,0:T(8,128)S(1)}, f32[5,64,128]{2,1,0:T(8,128)}, u32[]{:S(2)}) copy-start(f32[5,64,128]{2,1,0:T(8,128)} %residual_ref.1) | copy-start | bytes 491524
  2.1 0.9 %copy-start.5 = (f32[5,64,128]{2,1,0:T(8,128)S(1)}, f32[5,64,128]{2,1,0:T(8,128)}, u32[]{:S(2)}) copy-start(f32[5,64,128]{2,1,0:T(8,128)} %speed_ref.2) | copy-start | bytes 491524
  3.0 0.8 %copy-start.7 = (f32[64,128]{1,0:T(8,128)S(1)}, f32[64,128]{1,0:T(8,128)}, u32[]{:S(2)}) copy-start(f32[64,128]{1,0:T(8,128)} %damp_ref.2) | copy-start | bytes 98308
  4.5 20.5 %copy-start.1 = (f32[5,5,64,128]{3,2,1,0:T(8,128)S(1)}, f32[5,5,64,128]{3,2,1,0:T(8,128)}, u32[]{:S(2)}) copy-start(f32[5,5,64,128]{3,2,1,0:T(8,128)} %middle_ref.1) | copy-start | bytes 2457604
  4.6 20.4 %copy-start.3 = (f32[5,64,128]{2,1,0:T(8,128)S(1)}, f32[5,64,128]{2,1,0:T(8,128)}, u32[]{:S(2)}) copy-start(f32[5,64,128]{2,1,0:T(8,128)} %speed_ref.3) | copy-start | bytes 491524
  4.6 20.4 %copy-start.6 = (f32[64,128]{1,0:T(8,128)S(1)}, f32[64,128]{1,0:T(8,128)}, u32[]{:S(2)}) copy-start(f32[64,128]{1,0:T(8,128)} %damp_ref.3) | copy-start | bytes 98308
  25.0 38.0 %copy-start.2 = (f32[5,5,64,128]{3,2,1,0:T(8,128)S(1)}, f32[5,5,64,128]{3,2,1,0:T(8,128)}, u32[]{:S(2)}) copy-start(f32[5,5,64,128]{3,2,1,0:T(8,128)} %right_ref.1) | copy-start | bytes 2457604
where the time goes:
time: 64.2 us; the launch traced here: 63.9 us
  blocking collectives  55.7 us (87%)
  Pallas kernels  4.36 us (7%)
  local copies, waits for them, and re-layouts  3.75 us (6%)
    all_to_all x1, blocking collectives, per_device(): lax.all_to_all(xi_send.reshape(loop, LANES // loop, LANES), 'xi', 0, 0, t...  22.1 us
    all_gather x1, blocking collectives, per_device(): eta_got = lax.all_gather(eta_send, 'eta', axis=0, tiled=True)  20.4 us
    all_to_all x1, blocking collectives, per_device(): lax.all_to_all(loop_send.reshape(loop, LANES // loop, LANES), 'xi', 0, 0,...  13.2 us
    pallas_call x4, Pallas kernels, run(): pl.pallas_call(kernel, out_shape=list(outs), in_specs=specs, out_specs=ou...  4.36 us
    unnamed x16, local copies, waits for them, and re-layouts  3.75 us

commit v1 on v0

--- a/solution.py
+++ b/solution.py
@@ -210,16 +210,11 @@
     return value_of([cols_ref[c, f, j] for c in range(5)], outside)
 
 
-def apply_cells(matrix_ref, values, out_ref):
-    for f in range(FIELDS):
-        total = matrix_ref[f, 0] * values[0]
-        for g in range(1, FIELDS):
-            total = total + matrix_ref[f, g] * values[g]
-        out_ref[f] = total
-
-
-def rim_rows(first, last):
-    return [first[0], first[1], last[0], last[1]]
+def mix(matrix_ref, f, values):
+    total = matrix_ref[f, 0] * values[0]
+    for g in range(1, FIELDS):
+        total = total + matrix_ref[f, g] * values[g]
+    return total
 
 
 def to_eta_rows(block):
@@ -235,15 +230,28 @@
 
 
 def eta_reduce_kernel(
-    residual_ref, left_ref, speed_ref, damp_ref,
+    residual_hbm, left_hbm, speed_hbm, damp_hbm,
     send_ref, cols_ref, meet0_ref, meet1_ref, meet2_ref,
-    work_ref, turned_ref, form_ref, mid_ref, small_ref,
+    residual_ref, left_ref, speed_ref, damp_ref, sems,
+    turned_ref, form_ref, mid_ref, small_ref,
 ):
-    apply_cells(left_ref, [residual_ref[g] for g in range(FIELDS)], work_ref)
-    for f in range(FIELDS):
-        turned_ref[f] = to_eta_rows(work_ref[f])
+    copies = [
+        pltpu.make_async_copy(damp_hbm, damp_ref, sems.at[0]),
+        pltpu.make_async_copy(speed_hbm, speed_ref, sems.at[1]),
+        pltpu.make_async_copy(residual_hbm, residual_ref, sems.at[2]),
+        pltpu.make_async_copy(left_hbm, left_ref, sems.at[3]),
+    ]
+    for copy in copies:
+        copy.start()
+    copies[0].wait()
+    turned_ref[2 * FIELDS] = to_eta_rows(damp_ref[...])
+    copies[1].wait()
+    for f in range(FIELDS):
         turned_ref[FIELDS + f] = to_eta_rows(speed_ref[f])
-    turned_ref[2 * FIELDS] = to_eta_rows(damp_ref[...])
+    copies[2].wait()
+    copies[3].wait()
+    for f in range(FIELDS):
+        turned_ref[f] = to_eta_rows(mix(left_ref, f, [residual_ref[g] for g in range(FIELDS)]))
 
     def cell(index, j):
         return turned_ref[index, pl.ds(SPAN * j, STEPS, stride=SPAN * STEPS), :]
@@ -344,7 +352,8 @@
                 eta_cols_ref, spread2_ref, f, j
             )
         solved.append(from_eta_rows(turned_ref[f]))
-    apply_cells(middle_ref, solved, mixed_ref)
+    for f in range(FIELDS):
+        mixed_ref[f] = mix(middle_ref, f, solved)
     reduce_sections(
         lambda f, j: mixed_ref[f, pl.ds(j, STEPS, stride=STEPS), :],
         lambda f, j: speed_ref[f, pl.ds(j, STEPS, stride=STEPS), :],
@@ -415,15 +424,29 @@
     square_ref[...] = jnp.zeros((LANES, LANES), jnp.float32)
     for x in range(4):
         square_ref[pl.ds(FIELDS * x, FIELDS), :] = terms[x]
-    send_ref[...] = jnp.transpose(square_ref[...])
+    square_ref[...] = jnp.transpose(square_ref[...])
+    devices = LANES // width
+    total = square_ref[pl.ds(0, devices, stride=width), :]
+    for part in range(1, width):
+        piece = square_ref[pl.ds(part, devices, stride=width), :]
+        total = total + pltpu.roll(piece, part * devices, 1)
+    send_ref[...] = total
 
 
 def xi_finish_kernel(
     got_ref, cols_ref, meet0_ref, meet1_ref, meet2_ref, right_ref,
-    out_ref,
-    square_ref, spread0_ref, spread1_ref, spread2_ref, solved_ref,
+    out_hbm,
+    square_ref, spread0_ref, spread1_ref, spread2_ref, solved_ref, out_ref, sems,
 ):
-    square_ref[...] = jnp.transpose(got_ref[...])
+    devices = got_ref.shape[0]
+    width = LANES // devices
+    got = got_ref[...]
+    square_ref[pl.ds(0, devices, stride=width), :] = got
+    for part in range(1, width):
+        square_ref[pl.ds(part, devices, stride=width), :] = pltpu.roll(
+            got, LANES - part * devices, 1
+        )
+    square_ref[...] = jnp.transpose(square_ref[...])
     outside = [square_ref[pl.ds(FIELDS * x, FIELDS), :] for x in range(4)]
     spread_tree(
         outside, (meet0_ref, meet1_ref, meet2_ref), (spread0_ref, spread1_ref, spread2_ref)
@@ -433,7 +456,13 @@
             solved_ref[f, pl.ds(j, STEPS, stride=STEPS), :] = section_values(
                 cols_ref, spread2_ref, f, j
             )
-    apply_cells(right_ref, [solved_ref[g] for g in range(FIELDS)], out_ref)
+    copies = []
+    for f in range(FIELDS):
+        out_ref[f] = mix(right_ref, f, [solved_ref[g] for g in range(FIELDS)])
+        copies.append(pltpu.make_async_copy(out_ref.at[f], out_hbm.at[f], sems.at[f]))
+        copies[f].start()
+    for copy in copies:
+        copy.wait()
 
 
 def shape(*dims):
@@ -454,37 +483,53 @@
 SPREADS = (vmem(4, 10, LANES), vmem(4, 20, LANES), vmem(4, 40, LANES))
 
 
-def call(kernel, outs, scratch, name, scalars=0):
-    def run(*args):
-        specs = [pl.BlockSpec(memory_space=pltpu.SMEM)] * scalars
-        specs += [pl.BlockSpec(memory_space=pltpu.VMEM)] * (len(args) - scalars)
-        out_specs = [pl.BlockSpec(memory_space=pltpu.VMEM)] * len(outs)
-        return pl.pallas_call(
-            kernel,
-            out_shape=list(outs),
-            in_specs=specs,
-            out_specs=out_specs,
-            scratch_shapes=list(scratch),
-            compiler_params=pltpu.CompilerParams(vmem_limit_bytes=24 * 2**20),
-            name=name,
-        )(*args)
-
-    return run
-
-
-def per_device(residual, left_eta, middle, right_xi, speed_eta, speed_xi, damping_eta, damping_xi):
-    fields, cells_xi, cells_local = residual.shape
-    eta_send, *eta_kept = call(
+ON_CHIP = pl.BlockSpec(memory_space=pltpu.VMEM)
+IN_PLACE = pl.BlockSpec(memory_space=pltpu.HBM)
+
+
+def call(kernel, in_specs, outs, out_specs, scratch, name):
+    return pl.pallas_call(
+        kernel,
+        out_shape=list(outs),
+        in_specs=in_specs,
+        out_specs=out_specs,
+        scratch_shapes=list(scratch),
+        compiler_params=pltpu.CompilerParams(vmem_limit_bytes=24 * 2**20),
+        name=name,
+    )
+
+
+def in_place(*arrays):
+    return [pltpu.with_memory_space_constraint(x, pltpu.HBM) for x in arrays]
+
+
+def eta_reduce(residual, left_eta, speed_eta, damping_eta):
+    fields, cells_xi, _ = residual.shape
+    return call(
         eta_reduce_kernel,
+        [IN_PLACE] * 4,
         (shape(SENT * FIELDS, LANES),) + KEPT,
-        (vmem(FIELDS, cells_xi, LANES), vmem(2 * FIELDS + 1, LANES, LANES)) + FORMS,
+        [ON_CHIP] * 5,
+        (
+            vmem(fields, cells_xi, LANES),
+            vmem(fields, fields, cells_xi, LANES),
+            vmem(fields, cells_xi, LANES),
+            vmem(cells_xi, LANES),
+            pltpu.SemaphoreType.DMA((4,)),
+            vmem(2 * FIELDS + 1, LANES, LANES),
+        )
+        + FORMS,
         "eta_reduce",
-    )(residual, left_eta, speed_eta, damping_eta)
-    eta_got = lax.all_gather(eta_send, "eta", axis=0, tiled=True)
-    place = lax.axis_index("eta").reshape(1).astype(jnp.int32)
-    xi_send, *xi_kept = call(
+    )(*in_place(residual, left_eta, speed_eta, damping_eta))
+
+
+def eta_finish(place, eta_got, eta_kept, middle, speed_xi, damping_xi):
+    cells_xi = damping_xi.shape[0]
+    return call(
         eta_finish_kernel,
+        [pl.BlockSpec(memory_space=pltpu.SMEM)] + [ON_CHIP] * 8,
         (shape(LANES, LANES),) + KEPT,
+        [ON_CHIP] * 5,
         FORMS
         + SPREADS
         + (
@@ -495,25 +540,51 @@
             vmem(LANES, LANES),
         ),
         "eta_finish",
-        scalars=1,
     )(place, eta_got, *eta_kept, middle, speed_xi, damping_xi)
+
+
+def xi_loop(xi_got, loop):
+    return call(
+        xi_loop_kernel,
+        [ON_CHIP],
+        (shape(loop, LANES),),
+        [ON_CHIP],
+        (vmem(LANES, LANES),),
+        "xi_loop",
+    )(xi_got)[0]
+
+
+def xi_finish(loop_got, xi_kept, right_xi):
+    fields, _, cells_xi, cells_local = right_xi.shape
+    return call(
+        xi_finish_kernel,
+        [ON_CHIP] * 6,
+        (shape(fields, cells_xi, cells_local),),
+        [IN_PLACE],
+        (vmem(LANES, LANES),)
+        + SPREADS
+        + (
+            vmem(FIELDS, cells_xi, LANES),
+            vmem(FIELDS, cells_xi, LANES),
+            pltpu.SemaphoreType.DMA((FIELDS,)),
+        ),
+        "xi_finish",
+    )(loop_got, *xi_kept, right_xi)[0]
+
+
+def per_device(residual, left_eta, middle, right_xi, speed_eta, speed_xi, damping_eta, damping_xi):
+    eta_send, *eta_kept = eta_reduce(residual, left_eta, speed_eta, damping_eta)
+    eta_got = lax.all_gather(eta_send, "eta", axis=0, tiled=True)
+    place = lax.axis_index("eta").reshape(1).astype(jnp.int32)
+    xi_send, *xi_kept = eta_finish(place, eta_got, eta_kept, middle, speed_xi, damping_xi)
     loop = lax.axis_size("xi")
     xi_got = lax.all_to_all(
         xi_send.reshape(loop, LANES // loop, LANES), "xi", 0, 0, tiled=True
     ).reshape(LANES, LANES)
-    (loop_send,) = call(xi_loop_kernel, (shape(LANES, LANES),), (vmem(LANES, LANES),), "xi_loop")(
-        xi_got
-    )
     loop_got = lax.all_to_all(
-        loop_send.reshape(loop, LANES // loop, LANES), "xi", 0, 0, tiled=True
-    ).reshape(LANES, LANES)
-    (increment,) = call(
-        xi_finish_kernel,
-        (shape(fields, cells_xi, cells_local),),
-        (vmem(LANES, LANES),) + SPREADS + (vmem(FIELDS, cells_xi, LANES),),
-        "xi_finish",
-    )(loop_got, *xi_kept, right_xi)
-    return increment
+        xi_loop(xi_got, loop).reshape(loop, 1, LANES), "xi", 0, 0, tiled=True
+    ).reshape(loop, LANES)
+    return xi_finish(loop_got, xi_kept, right_xi)
 
 
 def solution(mesh):

time: 64.2 us -> 61.5 us (0.958)
  local copies, waits for them, and re-layouts: 3.75 us -> 0.02 us
  Pallas kernels: 4.36 us -> 5.71 us
    unnamed x16 -> x8, local copies, waits for them, and re-layouts: 3.75 us -> 0.02 us
    pallas_call x4, Pallas kernels: 4.36 us -> 5.71 us  [the longest x1 1.99 us: eta_reduce(): call(eta_reduce_kernel, [IN_PLACE] * 4, (shape(SENT * FIELDS, LANES),) +...]
where the time goes in v1:
time: 61.5 us; the launch traced here: 61.3 us
  blocking collectives  55.5 us (90%)
  Pallas kernels  5.71 us (9%)
    all_to_all x1, blocking collectives, per_device(): lax.all_to_all(xi_send.reshape(loop, LANES // loop, LANES), 'xi', 0, 0, t...  22.1 us
    all_gather x1, blocking collectives, per_device(): eta_got = lax.all_gather(eta_send, 'eta', axis=0, tiled=True)  20.4 us
    all_to_all x1, blocking collectives, per_device(): lax.all_to_all(xi_loop(xi_got, loop).reshape(loop, 1, LANES), 'xi', 0, 0,...  12.9 us
    pallas_call x1, Pallas kernels, eta_reduce(): call(eta_reduce_kernel, [IN_PLACE] * 4, (shape(SENT * FIELDS, LANES),) +...  1.99 us
    pallas_call x1, Pallas kernels, eta_finish(): call(eta_finish_kernel, [pl.BlockSpec(memory_space=pltpu.SMEM)] + [ON_CHI...  1.75 us

profile of v1, /device:TPU:2, one launch (start us, length us, event | category | flops | bytes accessed | tf_op | source)
XLA Modules:
  0.0 61.3 jit_solution(13704499001029811269)
XLA Ops:
  0.0 2.0 %eta_reduce.1 = (f32[120,128]{1,0:T(8,128)S(1)}, f32[5,5,8,8,128]{4,3,2,1,0:T(8,128)S(1)}, f32[20,20,128]{2,1,0:T(8,128)S(1)}, f32[20,10,128]{2,1,0:T(8,128)S(1)}, f32[20,5,128]{2,1,0:T(8,128)S(1)}) custom-call(f32[5,64,128]{2,1,0:T(8,128)} %residual_hbm.1, f32[5,5,64,128]{3,2,1,0:T(8,128)} %left_hbm.1, f32[5,64,128]{2,1,0:T(8,128)} %speed_hbm.1, ...), custom_call_target="tpu_custom_call" | custom-call | tf_op jit(solution)/shard_map/eta_reduce/pallas_call | solution.py:508
  2.0 0.0 copy-start
  2.0 0.0 copy-start.2
  2.0 0.0 copy-start.3
  2.0 20.4 %all_gather.3.got_ref = f32[1920,128]{1,0:T(8,128)S(1)} all-gather(f32[120,128]{1,0:T(8,128)S(1)} %get-tuple-element.15), channel_id=1, replica_groups=mesh['xi'=32,'eta'=16] {'eta'}, dimensions={0}, use_global_device_ids=true | all-gather | bytes 1044480 | tf_op jit(solution)/shard_map/all_gather | solution.py:577
  22.4 0.0 copy-done
  22.5 0.0 copy-done.2
  22.5 0.0 copy-done.3
  22.5 0.0 copy-start.1
  22.5 1.8 %eta_finish.1 = (f32[128,128]{1,0:T(8,128)S(1)}, f32[5,5,8,8,128]{4,3,2,1,0:T(8,128)S(1)}, f32[20,20,128]{2,1,0:T(8,128)S(1)}, f32[20,10,128]{2,1,0:T(8,128)S(1)}, f32[20,5,128]{2,1,0:T(8,128)S(1)}) custom-call(s32[1]{0:T(128)} %bitcast.place_ref, f32[1920,128]{1,0:T(8,128)S(1)} %all_gather.3.got_ref, ...), custom_call_target="tpu_custom_call" | custom-call | tf_op jit(solution)/shard_map/eta_finish/pallas_call | solution.py:528
  24.2 22.1 %all_to_all.10 = f32[32,4,128]{2,1,0:T(4,128)S(1)} all-to-all(f32[32,4,128]{2,1,0:T(4,128)S(1)} %bitcast.10), channel_id=1, replica_groups=mesh['xi'=32,'eta'=16] {'xi'}, dimensions={0} | all-to-all | bytes 131072 | tf_op jit(solution)/shard_map/all_to_all | solution.py:581
  46.3 1.0 %xi_loop.1 = f32[32,128]{1,0:T(8,128)S(1)} custom-call(f32[128,128]{1,0:T(8,128)S(1)} %bitcast.7), custom_call_target="tpu_custom_call" | custom-call | tf_op jit(solution)/shard_map/xi_loop/pallas_call | solution.py:547
  47.3 12.9 %all_to_all.11 = f32[32,1,128]{2,1,0:T(1,128)S(1)} all-to-all(f32[32,1,128]{2,1,0:T(1,128)S(1)} %bitcast.9), channel_id=1, replica_groups=mesh['xi'=32,'eta'=16] {'xi'}, dimensions={0} | all-to-all | bytes 32768 | tf_op jit(solution)/shard_map/all_to_all | solution.py:584
  60.3 0.0 copy-done.1
  60.3 1.0 %xi_finish.1 = f32[5,64,128]{2,1,0:T(8,128)} custom-call(f32[32,128]{1,0:T(8,128)S(1)} %bitcast.8, f32[5,5,8,8,128]{4,3,2,1,0:T(8,128)S(1)} %get-tuple-element.21.cols_ref, f32[20,20,128]{2,1,0:T(8,128)S(1)} %get-tuple-element.22.meet0_ref, f32[20,10,128]{2,1,0:T(8,128)S(1)} %get-tuple-element.23.meet1_ref, f32[20,5,128]{2,1,0:T(8,128)S(1)} %get-tuple-element.24.meet2_ref, ...), custom_call_target="tpu_custom_call" | custom-call | tf_op jit(solution)/shard_map/xi_finish/pallas_call | solution.py:559
Async XLA Ops:
  2.0 20.5 %copy-start = (f32[5,5,64,128]{3,2,1,0:T(8,128)S(1)}, f32[5,5,64,128]{3,2,1,0:T(8,128)}, u32[]{:S(2)}) copy-start(f32[5,5,64,128]{3,2,1,0:T(8,128)} %middle_ref.1) | copy-start | bytes 2457604
  2.0 20.4 %copy-start.2 = (f32[5,64,128]{2,1,0:T(8,128)S(1)}, f32[5,64,128]{2,1,0:T(8,128)}, u32[]{:S(2)}) copy-start(f32[5,64,128]{2,1,0:T(8,128)} %speed_ref.1) | copy-start | bytes 491524
  2.0 20.4 %copy-start.3 = (f32[64,128]{1,0:T(8,128)S(1)}, f32[64,128]{1,0:T(8,128)}, u32[]{:S(2)}) copy-start(f32[64,128]{1,0:T(8,128)} %damp_ref.1) | copy-start | bytes 98308
  22.5 37.8 %copy-start.1 = (f32[5,5,64,128]{3,2,1,0:T(8,128)S(1)}, f32[5,5,64,128]{3,2,1,0:T(8,128)}, u32[]{:S(2)}) copy-start(f32[5,5,64,128]{3,2,1,0:T(8,128)} %right_ref.1) | copy-start | bytes 2457604

commit v2 on v1

--- a/solution.py
+++ b/solution.py
@@ -13,6 +13,16 @@
 LANES = 128
 FORM = 20
 SENT = 24
+
+
+ROUNDING = 2.0**-24
+
+
+def inverse_parts(m00, m01, m10, m11):
+    both = m00 * m11
+    determinant = both - m01 * m10
+    inv = 1.0 / jnp.where(determinant == 0.0, both * ROUNDING, determinant)
+    return m00 * inv, m01 * inv, m10 * inv, m11 * inv
 
 
 def merge(low, high):
@@ -24,8 +34,7 @@
     m01 = -(l00 * u01 + l01 * u11)
     m10 = -(l10 * u00 + l11 * u10)
     m11 = 1.0 - l10 * u01 - l11 * u11
-    inv = 1.0 / (m00 * m11 - m01 * m10)
-    m00, m01, m10, m11 = m00 * inv, m01 * inv, m10 * inv, m11 * inv
+    m00, m01, m10, m11 = inverse_parts(m00, m01, m10, m11)
     r0 = [b_p0[0] - l00 * a_q0[0] - l01 * a_q1[0]]
     r1 = [b_p1[0] - l10 * a_q0[0] - l11 * a_q1[0]]
     for c in (1, 2):
@@ -67,8 +76,7 @@
     first, last = rows[0], rows[3]
     e00, e01 = 1.0 + first[1], first[4]
     e10, e11 = last[1], 1.0 + last[4]
-    inv = 1.0 / (e00 * e11 - e01 * e10)
-    e00, e01, e10, e11 = e00 * inv, e01 * inv, e10 * inv, e11 * inv
+    e00, e01, e10, e11 = inverse_parts(e00, e01, e10, e11)
     new_first = [e11 * s - e01 * t for s, t in zip(first, last)]
     new_last = [e00 * t - e10 * s for s, t in zip(first, last)]
     inner = [
@@ -402,23 +410,22 @@
     while width * distance < LANES:
         form, unused = merge(form, [from_above(x, distance) for x in form])
         distance = 2 * distance
-    unknown = [[None] * 5 for _ in range(4)]
-    for x in range(4):
-        k, a, b, c, d = form[5 * x : 5 * x + 5]
-        unknown[x] = [c, d, a, b, k]
-        unknown[x][x] = 1.0 + unknown[x][x]
-    for pivot in range(4):
-        inv = 1.0 / unknown[pivot][pivot]
-        scaled = [unknown[pivot][c] * inv for c in range(pivot + 1, 5)]
-        for x in range(4):
-            if x == pivot:
-                continue
-            factor = unknown[x][pivot]
-            for c in range(pivot + 1, 5):
-                unknown[x][c] = unknown[x][c] - factor * scaled[c - pivot - 1]
-        for c in range(pivot + 1, 5):
-            unknown[pivot][c] = scaled[c - pivot - 1]
-    p0, p1, l0, l1 = (unknown[x][4] for x in range(4))
+    rows = [form[5 * x : 5 * x + 5] for x in range(4)]
+    e00, e01, e10, e11 = inverse_parts(
+        1.0 + rows[0][3], rows[0][4], rows[1][3], 1.0 + rows[1][4]
+    )
+    first = [e11 * rows[0][c] - e01 * rows[1][c] for c in range(3)]
+    second = [e00 * rows[1][c] - e10 * rows[0][c] for c in range(3)]
+    left = [
+        [row[c] - row[3] * first[c] - row[4] * second[c] for c in range(3)] for row in rows[2:]
+    ]
+    e00, e01, e10, e11 = inverse_parts(
+        1.0 + left[0][1], left[0][2], left[1][1], 1.0 + left[1][2]
+    )
+    l0 = e11 * left[0][0] - e01 * left[1][0]
+    l1 = e00 * left[1][0] - e10 * left[0][0]
+    p0 = first[0] - first[1] * l0 - first[2] * l1
+    p1 = second[0] - second[1] * l0 - second[2] * l1
     r0, r1 = from_above(p0, 1), from_above(p1, 1)
     terms = rim_terms([l0, l1, r0, r1], p0, from_above(l1, 1), *rims)
     square_ref[...] = jnp.zeros((LANES, LANES), jnp.float32)

time: 61.5 us -> 61.5 us (level)
  no operation moved by 1% of the time
where the time goes in v2:
time: 61.5 us; the launch traced here: 61.3 us
  blocking collectives  55.5 us (90%)
  Pallas kernels  5.73 us (9%)
    all_to_all x1, blocking collectives, per_device(): lax.all_to_all(xi_send.reshape(loop, LANES // loop, LANES), 'xi', 0, 0, t...  22.1 us
    all_gather x1, blocking collectives, per_device(): eta_got = lax.all_gather(eta_send, 'eta', axis=0, tiled=True)  20.4 us
    all_to_all x1, blocking collectives, per_device(): lax.all_to_all(xi_loop(xi_got, loop).reshape(loop, 1, LANES), 'xi', 0, 0,...  12.9 us
    pallas_call x1, Pallas kernels, eta_reduce(): call(eta_reduce_kernel, [IN_PLACE] * 4, (shape(SENT * FIELDS, LANES),) +...  1.99 us
    pallas_call x1, Pallas kernels, eta_finish(): call(eta_finish_kernel, [pl.BlockSpec(memory_space=pltpu.SMEM)] + [ON_CHI...  1.76 us

profile of v2, /device:TPU:2, one launch (start us, length us, event | category | flops | bytes accessed | tf_op | source)
XLA Modules:
  0.0 61.3 jit_solution(8589104211099269374)
XLA Ops:
  0.0 2.0 %eta_reduce.1 = (f32[120,128]{1,0:T(8,128)S(1)}, f32[5,5,8,8,128]{4,3,2,1,0:T(8,128)S(1)}, f32[20,20,128]{2,1,0:T(8,128)S(1)}, f32[20,10,128]{2,1,0:T(8,128)S(1)}, f32[20,5,128]{2,1,0:T(8,128)S(1)}) custom-call(f32[5,64,128]{2,1,0:T(8,128)} %residual_hbm.1, f32[5,5,64,128]{3,2,1,0:T(8,128)} %left_hbm.1, f32[5,64,128]{2,1,0:T(8,128)} %speed_hbm.1, ...), custom_call_target="tpu_custom_call" | custom-call | tf_op jit(solution)/shard_map/eta_reduce/pallas_call | solution.py:515
  2.0 0.0 copy-start
  2.0 0.0 copy-start.2
  2.0 0.0 copy-start.3
  2.0 20.4 %all_gather.3.got_ref = f32[1920,128]{1,0:T(8,128)S(1)} all-gather(f32[120,128]{1,0:T(8,128)S(1)} %get-tuple-element.15), channel_id=1, replica_groups=mesh['xi'=32,'eta'=16] {'eta'}, dimensions={0}, use_global_device_ids=true | all-gather | bytes 1044480 | tf_op jit(solution)/shard_map/all_gather | solution.py:584
  22.5 0.0 copy-done
  22.5 0.0 copy-done.2
  22.5 0.0 copy-done.3
  22.5 0.0 copy-start.1
  22.5 1.8 %eta_finish.1 = (f32[128,128]{1,0:T(8,128)S(1)}, f32[5,5,8,8,128]{4,3,2,1,0:T(8,128)S(1)}, f32[20,20,128]{2,1,0:T(8,128)S(1)}, f32[20,10,128]{2,1,0:T(8,128)S(1)}, f32[20,5,128]{2,1,0:T(8,128)S(1)}) custom-call(s32[1]{0:T(128)} %bitcast.place_ref, f32[1920,128]{1,0:T(8,128)S(1)} %all_gather.3.got_ref, ...), custom_call_target="tpu_custom_call" | custom-call | tf_op jit(solution)/shard_map/eta_finish/pallas_call | solution.py:535
  24.2 22.1 %all_to_all.10 = f32[32,4,128]{2,1,0:T(4,128)S(1)} all-to-all(f32[32,4,128]{2,1,0:T(4,128)S(1)} %bitcast.10), channel_id=1, replica_groups=mesh['xi'=32,'eta'=16] {'xi'}, dimensions={0} | all-to-all | bytes 131072 | tf_op jit(solution)/shard_map/all_to_all | solution.py:588
  46.4 1.0 %xi_loop.1 = f32[32,128]{1,0:T(8,128)S(1)} custom-call(f32[128,128]{1,0:T(8,128)S(1)} %bitcast.7), custom_call_target="tpu_custom_call" | custom-call | tf_op jit(solution)/shard_map/xi_loop/pallas_call | solution.py:554
  47.3 12.9 %all_to_all.11 = f32[32,1,128]{2,1,0:T(1,128)S(1)} all-to-all(f32[32,1,128]{2,1,0:T(1,128)S(1)} %bitcast.9), channel_id=1, replica_groups=mesh['xi'=32,'eta'=16] {'xi'}, dimensions={0} | all-to-all | bytes 32768 | tf_op jit(solution)/shard_map/all_to_all | solution.py:591
  60.3 0.0 copy-done.1
  60.3 1.0 %xi_finish.1 = f32[5,64,128]{2,1,0:T(8,128)} custom-call(f32[32,128]{1,0:T(8,128)S(1)} %bitcast.8, f32[5,5,8,8,128]{4,3,2,1,0:T(8,128)S(1)} %get-tuple-element.21.cols_ref, f32[20,20,128]{2,1,0:T(8,128)S(1)} %get-tuple-element.22.meet0_ref, f32[20,10,128]{2,1,0:T(8,128)S(1)} %get-tuple-element.23.meet1_ref, f32[20,5,128]{2,1,0:T(8,128)S(1)} %get-tuple-element.24.meet2_ref, ...), custom_call_target="tpu_custom_call" | custom-call | tf_op jit(solution)/shard_map/xi_finish/pallas_call | solution.py:566
Async XLA Ops:
  2.0 20.5 %copy-start = (f32[5,5,64,128]{3,2,1,0:T(8,128)S(1)}, f32[5,5,64,128]{3,2,1,0:T(8,128)}, u32[]{:S(2)}) copy-start(f32[5,5,64,128]{3,2,1,0:T(8,128)} %middle_ref.1) | copy-start | bytes 2457604
  2.0 20.4 %copy-start.2 = (f32[5,64,128]{2,1,0:T(8,128)S(1)}, f32[5,64,128]{2,1,0:T(8,128)}, u32[]{:S(2)}) copy-start(f32[5,64,128]{2,1,0:T(8,128)} %speed_ref.1) | copy-start | bytes 491524
  2.0 20.4 %copy-start.3 = (f32[64,128]{1,0:T(8,128)S(1)}, f32[64,128]{1,0:T(8,128)}, u32[]{:S(2)}) copy-start(f32[64,128]{1,0:T(8,128)} %damp_ref.1) | copy-start | bytes 98308
  22.5 37.8 %copy-start.1 = (f32[5,5,64,128]{3,2,1,0:T(8,128)S(1)}, f32[5,5,64,128]{3,2,1,0:T(8,128)}, u32[]{:S(2)}) copy-start(f32[5,5,64,128]{3,2,1,0:T(8,128)} %right_ref.1) | copy-start | bytes 2457604

commit v3 on v2

--- a/solution.py
+++ b/solution.py
@@ -246,8 +246,8 @@
     copies = [
         pltpu.make_async_copy(damp_hbm, damp_ref, sems.at[0]),
         pltpu.make_async_copy(speed_hbm, speed_ref, sems.at[1]),
-        pltpu.make_async_copy(residual_hbm, residual_ref, sems.at[2]),
-        pltpu.make_async_copy(left_hbm, left_ref, sems.at[3]),
+        pltpu.make_async_copy(left_hbm, left_ref, sems.at[2]),
+        pltpu.make_async_copy(residual_hbm, residual_ref, sems.at[3]),
     ]
     for copy in copies:
         copy.start()

time: 61.5 us -> 61.4 us (level)
  no operation moved by 1% of the time
where the time goes in v3:
time: 61.4 us; the launch traced here: 61.2 us
  blocking collectives  55.5 us (90%)
  Pallas kernels  5.66 us (9%)
    all_to_all x1, blocking collectives, per_device(): lax.all_to_all(xi_send.reshape(loop, LANES // loop, LANES), 'xi', 0, 0, t...  22.1 us
    all_gather x1, blocking collectives, per_device(): eta_got = lax.all_gather(eta_send, 'eta', axis=0, tiled=True)  20.4 us
    all_to_all x1, blocking collectives, per_device(): lax.all_to_all(xi_loop(xi_got, loop).reshape(loop, 1, LANES), 'xi', 0, 0,...  12.9 us
    pallas_call x1, Pallas kernels, eta_reduce(): call(eta_reduce_kernel, [IN_PLACE] * 4, (shape(SENT * FIELDS, LANES),) +...  1.92 us
    pallas_call x1, Pallas kernels, eta_finish(): call(eta_finish_kernel, [pl.BlockSpec(memory_space=pltpu.SMEM)] + [ON_CHI...  1.76 us

profile of v3, /device:TPU:2, one launch (start us, length us, event | category | flops | bytes accessed | tf_op | source)
XLA Modules:
  0.0 61.2 jit_solution(11926693994179632469)
XLA Ops:
  0.0 1.9 %eta_reduce.1 = (f32[120,128]{1,0:T(8,128)S(1)}, f32[5,5,8,8,128]{4,3,2,1,0:T(8,128)S(1)}, f32[20,20,128]{2,1,0:T(8,128)S(1)}, f32[20,10,128]{2,1,0:T(8,128)S(1)}, f32[20,5,128]{2,1,0:T(8,128)S(1)}) custom-call(f32[5,64,128]{2,1,0:T(8,128)} %residual_hbm.1, f32[5,5,64,128]{3,2,1,0:T(8,128)} %left_hbm.1, f32[5,64,128]{2,1,0:T(8,128)} %speed_hbm.1, ...), custom_call_target="tpu_custom_call" | custom-call | tf_op jit(solution)/shard_map/eta_reduce/pallas_call | solution.py:515
  1.9 0.0 copy-start
  1.9 0.0 copy-start.2
  2.0 0.0 copy-start.3
  2.0 20.4 %all_gather.3.got_ref = f32[1920,128]{1,0:T(8,128)S(1)} all-gather(f32[120,128]{1,0:T(8,128)S(1)} %get-tuple-element.15), channel_id=1, replica_groups=mesh['xi'=32,'eta'=16] {'eta'}, dimensions={0}, use_global_device_ids=true | all-gather | bytes 1044480 | tf_op jit(solution)/shard_map/all_gather | solution.py:584
  22.4 0.0 copy-done
  22.4 0.0 copy-done.2
  22.4 0.0 copy-done.3
  22.4 0.0 copy-start.1
  22.4 1.8 %eta_finish.1 = (f32[128,128]{1,0:T(8,128)S(1)}, f32[5,5,8,8,128]{4,3,2,1,0:T(8,128)S(1)}, f32[20,20,128]{2,1,0:T(8,128)S(1)}, f32[20,10,128]{2,1,0:T(8,128)S(1)}, f32[20,5,128]{2,1,0:T(8,128)S(1)}) custom-call(s32[1]{0:T(128)} %bitcast.place_ref, f32[1920,128]{1,0:T(8,128)S(1)} %all_gather.3.got_ref, ...), custom_call_target="tpu_custom_call" | custom-call | tf_op jit(solution)/shard_map/eta_finish/pallas_call | solution.py:535
  24.2 22.1 %all_to_all.10 = f32[32,4,128]{2,1,0:T(4,128)S(1)} all-to-all(f32[32,4,128]{2,1,0:T(4,128)S(1)} %bitcast.10), channel_id=1, replica_groups=mesh['xi'=32,'eta'=16] {'xi'}, dimensions={0} | all-to-all | bytes 131072 | tf_op jit(solution)/shard_map/all_to_all | solution.py:588
  46.3 1.0 %xi_loop.1 = f32[32,128]{1,0:T(8,128)S(1)} custom-call(f32[128,128]{1,0:T(8,128)S(1)} %bitcast.7), custom_call_target="tpu_custom_call" | custom-call | tf_op jit(solution)/shard_map/xi_loop/pallas_call | solution.py:554
  47.3 12.9 %all_to_all.11 = f32[32,1,128]{2,1,0:T(1,128)S(1)} all-to-all(f32[32,1,128]{2,1,0:T(1,128)S(1)} %bitcast.9), channel_id=1, replica_groups=mesh['xi'=32,'eta'=16] {'xi'}, dimensions={0} | all-to-all | bytes 32768 | tf_op jit(solution)/shard_map/all_to_all | solution.py:591
  60.2 0.0 copy-done.1
  60.2 1.0 %xi_finish.1 = f32[5,64,128]{2,1,0:T(8,128)} custom-call(f32[32,128]{1,0:T(8,128)S(1)} %bitcast.8, f32[5,5,8,8,128]{4,3,2,1,0:T(8,128)S(1)} %get-tuple-element.21.cols_ref, f32[20,20,128]{2,1,0:T(8,128)S(1)} %get-tuple-element.22.meet0_ref, f32[20,10,128]{2,1,0:T(8,128)S(1)} %get-tuple-element.23.meet1_ref, f32[20,5,128]{2,1,0:T(8,128)S(1)} %get-tuple-element.24.meet2_ref, ...), custom_call_target="tpu_custom_call" | custom-call | tf_op jit(solution)/shard_map/xi_finish/pallas_call | solution.py:566
Async XLA Ops:
  1.9 20.5 %copy-start = (f32[5,5,64,128]{3,2,1,0:T(8,128)S(1)}, f32[5,5,64,128]{3,2,1,0:T(8,128)}, u32[]{:S(2)}) copy-start(f32[5,5,64,128]{3,2,1,0:T(8,128)} %middle_ref.1) | copy-start | bytes 2457604
  1.9 20.4 %copy-start.2 = (f32[5,64,128]{2,1,0:T(8,128)S(1)}, f32[5,64,128]{2,1,0:T(8,128)}, u32[]{:S(2)}) copy-start(f32[5,64,128]{2,1,0:T(8,128)} %speed_ref.1) | copy-start | bytes 491524
  2.0 20.4 %copy-start.3 = (f32[64,128]{1,0:T(8,128)S(1)}, f32[64,128]{1,0:T(8,128)}, u32[]{:S(2)}) copy-start(f32[64,128]{1,0:T(8,128)} %damp_ref.1) | copy-start | bytes 98308
  22.4 37.8 %copy-start.1 = (f32[5,5,64,128]{3,2,1,0:T(8,128)S(1)}, f32[5,5,64,128]{3,2,1,0:T(8,128)}, u32[]{:S(2)}) copy-start(f32[5,5,64,128]{3,2,1,0:T(8,128)} %right_ref.1) | copy-start | bytes 2457604
